TPU v7x, 32 devices: a whole 2x2x4 slice. The times are simulated.
32 devices in a mesh: bal: 8 (over z, x), seq: 4 (over y, core).
Axes of the slice: x: 2, y: 2, z: 4, core: 2. Of those that a mesh axis runs over, the one named last changes fastest.
Arguments:
- tokens: bfloat16 [128, 64, 5120], P('bal', 'seq'), may hold values from -6 to 6
- w_qkv: bfloat16 [5120, 24, 384], P('bal', 'seq')
- q_gain: float32 [24, 128], P('seq')
- k_gain: float32 [24, 128], P('seq')
- modulation: float32 [8, 4, 2, 5120], P('bal'), may hold values from -3 to 3
- tile_owner: int32 [128], P('bal'), may hold values from 0 to 7, as said below
- clip_dims: int32 [8, 4, 3], P('bal'), may hold values from 0 to 4, as said below
Outputs:
- attn_out: bfloat16 [128, 64, 3072], P('bal', 'seq')
Inputs may be any that keep to these rules, and one draw needn't show every extreme that they name: `tile_owner`: each owner is named by exactly 16 tiles. The 16 tiles of one bal index name any owner at most 2 times, and in every draw some owner exactly 2 times. `clip_dims`: for each owner the clips' products f h w add up to 16; entries after its last clip are 0; a clip spans at most 2 tile frames, 3 tile rows and 4 tile columns and has 4 tiles or more.
All inputs are finite; a program needn't handle non-finite values.
Results may differ from a plain program's by a relative error of at most 0.006.
Values may be sent and summed in bfloat16 or wider, within the bound.
No kernel may reach another device: no remote copies, remote signals or barrier semaphores. Data moves between devices by JAX's collectives and lax.ppermute only.
A program may use at most 128 MiB of HBM per device.

v0:
```python
import jax
import jax.numpy as jnp
from jax import lax
from jax.sharding import PartitionSpec as P

HEADS = 24
TILES_OWN = 16
eps_norm = 1e-06
score_fill = -1e30


def tile_layout(clip_shape):
    frames_of = clip_shape[:, 0]
    rows_of = clip_shape[:, 1]
    cols_of = clip_shape[:, 2]
    clip_sizes = frames_of * rows_of * cols_of
    clip_ends = jnp.cumsum(clip_sizes)
    clip_starts = clip_ends - clip_sizes
    local_index = jnp.arange(TILES_OWN, dtype=jnp.int32)
    member = jnp.sum((local_index[:, None] >= clip_ends[None, :]).astype(jnp.int32), axis=1)
    onehot = member[:, None] == jnp.arange(clip_shape.shape[0], dtype=jnp.int32)[None, :]

    def select_clip(values):
        return jnp.sum(jnp.where(onehot, values[None, :], 0), axis=1)

    offset = local_index - select_clip(clip_starts)
    height = jnp.maximum(select_clip(rows_of), 1)
    width_tiles = jnp.maximum(select_clip(cols_of), 1)
    frame_index = offset // (height * width_tiles)
    row_index = offset // width_tiles % height
    column = offset % width_tiles

    def within_one(coords):
        return jnp.abs(coords[:, None] - coords[None, :]) <= 1

    tile_mask = (
        (member[:, None] == member[None, :])
        & within_one(frame_index)
        & within_one(row_index)
        & within_one(column)
    )
    return (onehot, tile_mask)


def clip_rows(onehot, mod_table):
    picked = jnp.sum(jnp.where(onehot[:, :, None, None], mod_table[None], 0.0), axis=1)
    return (picked[:, 0], picked[:, 1])


def modulate(pieces, shift_rows, scale_rows):
    values = pieces.astype(jnp.float32)
    center = jnp.mean(values, axis=-1, keepdims=True)
    spread = jnp.mean(jnp.square(values - center), axis=-1, keepdims=True)
    normal = (values - center) * lax.rsqrt(spread + eps_norm)
    return (normal * (1.0 + scale_rows[:, None, :]) + shift_rows[:, None, :]).astype(jnp.bfloat16)


def attend(q_block, key_rows, values, block_mask):
    scores = jnp.einsum(
        "qhd,khd->hqk", q_block, key_rows, preferred_element_type=jnp.float32
    ) * key_rows.shape[2] ** (-0.5)
    scores = jnp.where(block_mask[None], scores, score_fill)
    largest = jnp.max(scores, axis=-1, keepdims=True)
    exp_scores = jnp.exp(scores - largest)
    totals = jnp.sum(exp_scores, axis=-1, keepdims=True)
    weights = (exp_scores / totals).astype(jnp.bfloat16)
    return jnp.einsum("hqk,khd->qhd", weights, values, preferred_element_type=jnp.float32)


def per_device(tokens, w_qkv, q_gain, k_gain, modulation, tile_owner, clip_dims):
    groups = lax.axis_size("bal")
    owned_tiles, piece_len, width_model = tokens.shape
    capacity = owned_tiles // min(groups, owned_tiles)
    slot_count = groups * capacity
    flat_weight = w_qkv.reshape(w_qkv.shape[0], -1)
    slot_ids = jnp.arange(slot_count, dtype=jnp.int32)
    earlier = jnp.arange(owned_tiles)[:, None] > jnp.arange(owned_tiles)[None, :]
    slot_rank = jnp.sum((tile_owner[:, None] == tile_owner[None, :]) & earlier, axis=1)
    target = tile_owner * capacity + slot_rank
    route_onehot = (slot_ids[:, None] == target[None, :]).astype(jnp.bfloat16)
    outbound = jnp.dot(
        route_onehot, tokens.reshape(owned_tiles, -1), preferred_element_type=jnp.float32
    ).astype(jnp.bfloat16)
    outbound = outbound.reshape(groups, capacity, piece_len, width_model)
    filled = jnp.sum(route_onehot, axis=1).reshape(groups, capacity)
    arrived, arrived_flags = (
        lax.all_to_all(outbound, "bal", split_axis=0, concat_axis=0, tiled=True),
        lax.all_to_all(filled, "bal", split_axis=0, concat_axis=0, tiled=True),
    )
    live_slots = arrived_flags.reshape(slot_count) > 0.5
    position = jnp.cumsum(live_slots.astype(jnp.int32)) - 1
    collect = ((jnp.arange(TILES_OWN)[:, None] == position[None, :]) & live_slots[None, :]).astype(
        jnp.bfloat16
    )
    compact = jnp.dot(
        collect, arrived.reshape(slot_count, -1), preferred_element_type=jnp.float32
    ).astype(jnp.bfloat16)
    compact = compact.reshape(TILES_OWN, piece_len, width_model)
    onehot, tile_mask = tile_layout(clip_dims[0])
    shift_rows, scale_rows = clip_rows(onehot, modulation[0])
    whole_tiles = lax.all_gather(compact, "seq", axis=1, tiled=True)
    normed = modulate(whole_tiles, shift_rows, scale_rows)
    tile_len = normed.shape[1]
    token_rows = normed.reshape(-1, width_model)
    total_tokens = token_rows.shape[0]
    per_dev_heads = q_gain.shape[0]
    projected = jnp.dot(
        token_rows,
        lax.all_gather(flat_weight, "bal", axis=0, tiled=True),
        preferred_element_type=jnp.float32,
    )
    projected = projected.reshape(total_tokens, per_dev_heads, 3, -1)
    query = projected[:, :, 0]
    keyed = projected[:, :, 1]
    valued = projected[:, :, 2].astype(jnp.bfloat16)
    sums_q, sums_k = lax.psum(
        (jnp.sum(jnp.square(query), axis=(1, 2)), jnp.sum(jnp.square(keyed), axis=(1, 2))), "seq"
    )
    features = HEADS * query.shape[2]
    q_normed = (
        query * lax.rsqrt(sums_q / features + eps_norm)[:, None, None] * q_gain[None]
    ).astype(jnp.bfloat16)
    k_normed = (
        keyed * lax.rsqrt(sums_k / features + eps_norm)[:, None, None] * k_gain[None]
    ).astype(jnp.bfloat16)
    token_mask = jnp.repeat(jnp.repeat(tile_mask, tile_len, axis=0), tile_len, axis=1)
    block_rows = min(512, total_tokens)
    outputs = []
    for block_start in range(0, total_tokens, block_rows):
        outputs.append(
            attend(
                q_normed[block_start : block_start + block_rows],
                k_normed,
                valued,
                token_mask[block_start : block_start + block_rows],
            )
        )
    attended = jnp.concatenate(outputs, axis=0).astype(jnp.bfloat16)
    head_major = attended.reshape(TILES_OWN, tile_len, -1)
    spread_back = jnp.dot(
        collect.T, head_major.reshape(TILES_OWN, -1), preferred_element_type=jnp.float32
    ).astype(jnp.bfloat16)
    spread_back = spread_back.reshape(groups, capacity, tile_len, -1)
    returned = lax.all_to_all(
        lax.all_to_all(spread_back, "bal", split_axis=0, concat_axis=0, tiled=True),
        "seq",
        split_axis=2,
        concat_axis=3,
        tiled=True,
    )
    result = jnp.dot(
        route_onehot.T, returned.reshape(slot_count, -1), preferred_element_type=jnp.float32
    ).astype(jnp.bfloat16)
    return result.reshape(owned_tiles, piece_len, -1)


def solution(mesh):
    return jax.shard_map(
        per_device,
        mesh=mesh,
        in_specs=(
            P("bal", "seq", None),
            P("bal", "seq", None),
            P("seq", None),
            P("seq", None),
            P("bal", None, None, None),
            P("bal"),
            P("bal", None, None),
        ),
        out_specs=P("bal", "seq", None),
        check_vma=False,
    )
```

profile of v0, /device:TPU:0, one launch (start us, length us, event | category | flops | bytes accessed | tf_op | source)
XLA Modules:
  0.0 808.7 jit_solution(5014179867423074362)
XLA Ops:
  8.9 7.3 all-to-all-start
  16.2 3.2 copy.84
  20.2 2.9 copy.85
  23.1 6.0 all-to-all-start.1
  29.6 58.5 %all-to-all-done.1 = bf16[8,2,16,5120]{3,2,1,0:T(8,128)(2,1)S(1)} async-done(((bf16[8,2,16,5120]{3,2,1,0:T(8,128)(2,1)}), bf16[8,2,16,5120]{3,2,1,0:T(8,128)(2,1)S(1)}, u32[]{:S(2)}, u32[]{:S(2)}) %all-to-all-start.1) | async-done | bytes 2621472 | tf_op jit(solution)/shard_map/all_to_all | solution.py:87
  90.3 2.9 copy.87
  93.9 3.5 copy.67
  101.4 61.3 %all-gather.3.cloned.1.call-done = bf16[16,64,5120]{2,1,0:T(8,128)(2,1)} async-done(((bf16[16,16,5120]{2,1,0:T(8,128)(2,1)}), bf16[16,64,5120]{2,1,0:T(8,128)(2,1)}) %all-gather.3.cloned.1.call-update) | async-done | bytes 10485776 | tf_op jit(solution)/shard_map/all_gather | solution.py:101
  162.7 5.6 convert_reduce_fusion
  169.6 2.8 fusion.4
  172.5 8.3 %fusion.7 = bf16[16,64,5120]{2,1,0:T(8,128)(2,1)} fusion(bf16[16,64,5120]{2,1,0:T(8,128)(2,1)S(1)} %copy-done, f32[16,5120]{1,0:T(8,128)S(1)} %get-tuple-element.16, f32[16,5120]{1,0:T(8,128)S(1)} %get-tuple-element.15, f32[16,64]{1,0:T(8,128)S(1)} %add_rsqrt_fusion, f32[16,64]{1,0:T(8,128)S(1)} %broadcast_multiply_fusion), kind=kLoop, calls=%fused_computation.13 | loop fusion | flops 31457280 | bytes 21635072 | tf_op jit(solution)/shard_map/convert_element_type | solution.py:55
  180.8 434.4 %all-gather.5.cloned.1.call-done = bf16[5120,2304]{0,1:T(8,128)(2,1)} async-done(((bf16[640,2304]{0,1:T(8,128)(2,1)}), bf16[5120,2304]{0,1:T(8,128)(2,1)}) %all-gather.5.cloned.1.call-update) | async-done | bytes 23592976 | tf_op jit(solution)/shard_map/all_gather | solution.py:109
  615.1 29.6 %fusion.53 = f32[1024,6,3,128]{0,3,2,1:T(8,128)S(1)} fusion(bf16[1024,5120,1,1]{1,0,3,2:T(8,128)(2,1)} %bitcast.70, bf16[6,3,128,5120]{3,2,1,0:T(8,128)(2,1)} %bitcast.86), kind=kOutput, calls=%fused_computation.106 | convolution fusion | flops 24159191040 | bytes 43515904 | tf_op jit(solution)/shard_map/dot_general | solution.py:107
  644.8 3.6 copy-done.1
  649.1 6.5 all-reduce
  658.0 8.4 %fusion.25 = f32[6,512,1024]{2,1,0:T(8,128)} fusion(bf16[1024,6,128]{0,2,1:T(8,128)(2,1)S(1)} %multiply_convert_fusion.1, f32[1024,6,3,128]{0,3,2,1:T(8,128)} %copy-done.1, f32[6,128]{1,0:T(8,128)S(1)} %copy-done.4, f32[1024]{0:T(1024)S(1)} %get-tuple-element.27), kind=kOutput, calls=%fused_computation.46 | convolution fusion | flops 807665664 | bytes 16523264 | tf_op jit(solution)/shard_map/qhd,khd->hqk/dot_general | solution.py:59
  666.5 6.5 fusion.23
  672.9 17.2 %fusion.52 = (f32[6,512]{1,0:T(8,128)S(1)}, f32[6,512,1024]{2,1,0:T(8,128)}) fusion(f32[6,512,1024]{2,1,0:T(8,128)} %fusion.25, pred[512,1024]{1,0:T(8,128)(4,1)S(1)} %copy.68), kind=kOutput, calls=%fused_computation.105 | output fusion | flops 18875392 | bytes 25702400 | tf_op jit(solution)/shard_map/sub | solution.py:64
  690.1 6.9 fusion.21
  697.0 16.5 %fusion.51 = (f32[6,512]{1,0:T(8,128)S(1)}, f32[6,512,1024]{2,1,0:T(8,128)}) fusion(f32[6,512,1024]{2,1,0:T(8,128)} %fusion.23, pred[512,1024]{1,0:T(8,128)(4,1)S(1)} %copy.71), kind=kOutput, calls=%fused_computation.104 | output fusion | flops 18875392 | bytes 25702400 | tf_op jit(solution)/shard_map/sub | solution.py:64
  713.6 6.9 fusion.22
  721.8 3.2 copy.74
  731.9 40.6 %all_to_all.35 = bf16[8,2,64,768]{3,1,2,0:T(2,128)(2,1)S(1)} all-to-all(bf16[8,2,64,768]{3,1,2,0:T(2,128)(2,1)S(1)} %copy.75), channel_id=1, replica_groups=mesh['bal'=8,'seq'=4] {'bal'}, dimensions={0} | all-to-all | bytes 3145728 | tf_op jit(solution)/shard_map/all_to_all | solution.py:145
  773.6 22.6 %all_to_all.36 = bf16[8,2,64,768]{3,1,0,2:T(2,128)(2,1)S(1)} all-to-all(bf16[8,2,64,768]{3,1,0,2:T(2,128)(2,1)S(1)} %copy.76), channel_id=1, replica_groups=mesh['bal'=8,'seq'=4] {'seq'}, dimensions={2} | all-to-all | bytes 3145728 | tf_op jit(solution)/shard_map/all_to_all | solution.py:144
  (75 shorter events, 29.1 us)
Async XLA Ops:
  8.9 14.2 %all-to-all-start = ((bf16[8,1,2]{2,1,0:T(2,128)(2,1)}), bf16[8,1,2]{2,1,0:T(2,128)(2,1)S(1)}, u32[]{:S(2)}, u32[]{:S(2)}) async-start(bf16[8,1,2]{2,1,0:T(2,128)(2,1)} %all_to_all.30), calls=%async_computation | async-start | bytes 8192 | tf_op jit(solution)/shard_map/all_to_all | solution.py:88
  23.1 64.9 %all-to-all-start.1 = ((bf16[8,2,16,5120]{3,2,1,0:T(8,128)(2,1)}), bf16[8,2,16,5120]{3,2,1,0:T(8,128)(2,1)S(1)}, u32[]{:S(2)}, u32[]{:S(2)}) async-start(bf16[8,2,16,5120]{3,2,1,0:T(8,128)(2,1)} %bitcast.27), calls=%async_computation.1 | async-start | bytes 5242880 | tf_op jit(solution)/shard_map/all_to_all | solution.py:87
  29.1 133.5 %all-gather.3.cloned.1.call-start = ((), (), s32[]{:S(2)}) async-start(), calls=%async_computation.4 | async-start | bytes 13107200 | tf_op jit(solution)/shard_map/all_gather | solution.py:101
  90.3 3.5 copy-start.2
  93.3 4.1 copy-start.6
  93.3 521.8 %all-gather.5.cloned.1.call-start = ((), (), s32[]{:S(2)}) async-start(), calls=%async_computation.5 | async-start | bytes 26542080 | tf_op jit(solution)/shard_map/all_gather | solution.py:109
  97.4 3.7 copy-start.3
  162.7 7.0 copy-start
  644.8 3.6 copy-start.1
  648.4 7.2 copy-start.5
  649.0 8.9 %copy-start.4 = (f32[6,128]{1,0:T(8,128)S(1)}, f32[6,128]{1,0:T(8,128)}, u32[]{:S(2)}) copy-start(f32[6,128]{1,0:T(8,128)} %param.10) | copy-start | bytes 9220
  655.6 10.8 %slice-start = ((s8[9437184]{0:T(1024)(128)(4,1)}), s8[4194304]{0:T(1024)(128)(4,1)S(1)}, s32[]{:S(2)}) async-start(s8[9437184]{0:T(1024)(128)(4,1)} %bitcast.67), calls=%async_computation.6 | async-start | bytes 8388608
  658.0 8.4 %slice-start.1 = ((s8[9437184]{0:T(1024)(128)(4,1)}), s8[4194304]{0:T(1024)(128)(4,1)S(1)}, s32[]{:S(2)}) async-start(s8[9437184]{0:T(1024)(128)(4,1)} %bitcast.67), calls=%async_computation.7 | async-start | bytes 8388608
  658.0 8.4 %slice-start.2 = ((s8[9437184]{0:T(1024)(128)(4,1)}), s8[1048576]{0:T(1024)(128)(4,1)S(1)}, s32[]{:S(2)}) async-start(s8[9437184]{0:T(1024)(128)(4,1)} %bitcast.67), calls=%async_computation.8 | async-start | bytes 2097152
Sparse Core Ops, SparseCore 0:
  93.4 69.2 all-gather.2
  164.2 450.8 all-gather.4
where the time goes:
time: 815 us; the launch traced here: 809 us
  waiting for transfers between devices  554 us (68%)
  blocking collectives  69.8 us (9%)
  matrix products  62.7 us (8%)
  other arithmetic  57.9 us (7%)
  local copies, waits for them, and re-layouts  36.1 us (4%)
  between operations  14.2 us (2%)
  starting transfers between devices  13.9 us (2%)
    all_gather x1, waiting for transfers between devices, per_device(): lax.all_gather(flat_weight, 'bal', axis=0, tiled=True)  434 us
    all_gather x1, waiting for transfers between devices, per_device(): whole_tiles = lax.all_gather(compact, 'seq', axis=1, tiled=True)  61.3 us
    all_to_all x1, waiting for transfers between devices, per_device(): lax.all_to_all(outbound, 'bal', split_axis=0, concat_axis=0, tiled=True)  58.5 us
    all_to_all x1, blocking collectives, per_device(): lax.all_to_all(spread_back, 'bal', split_axis=0, concat_axis=0, tiled=True)  40.6 us
    sub x2, other arithmetic, attend(): exp_scores = jnp.exp(scores - largest)  33.7 us
    dot_general x1, matrix products, per_device(): jnp.dot(token_rows, lax.all_gather(flat_weight, 'bal', axis=0, tiled=True...  29.6 us
    all_to_all x1, blocking collectives, per_device(): lax.all_to_all(lax.all_to_all(spread_back, 'bal', split_axis=0, concat_ax...  22.6 us
    unnamed x28, local copies, waits for them, and re-layouts  21.4 us
  transfers between devices with their start and end apart: 4, of which 3 were waited for; matrix products, arithmetic and copies ran while one was open for 4% of the time, Pallas kernels for 0%

commit v1 on v0

--- a/solution.py
+++ b/solution.py
@@ -7,6 +7,28 @@
 TILES_OWN = 16
 eps_norm = 1e-06
 score_fill = -1e30
+
+
+def laid_out(parts, dim):
+    parts = jnp.moveaxis(parts, 0, dim)
+    shape = parts.shape
+    return parts.reshape(*shape[:dim], shape[dim] * shape[dim + 1], *shape[dim + 2 :])
+
+
+def ring_gather(x, axis, dim):
+    peers = lax.axis_size(axis)
+    pairs = [(i, (i + 1) % peers) for i in range(peers)]
+    back = [(b, a) for a, b in pairs]
+    lower, upper = ([], [])
+    for step in range(peers - 1):
+        if step % 2 == 0:
+            lower.append(lax.ppermute(lower[-1] if lower else x, axis, pairs))
+        else:
+            upper.append(lax.ppermute(upper[-1] if upper else x, axis, back))
+    pieces = jnp.stack([*lower[::-1], x, *upper])
+    shift = lax.axis_index(axis) - len(lower)
+    pieces = pieces[(jnp.arange(peers) - shift) % peers]
+    return laid_out(pieces, dim)
 
 
 def tile_layout(clip_shape):
@@ -105,9 +127,7 @@
     total_tokens = token_rows.shape[0]
     per_dev_heads = q_gain.shape[0]
     projected = jnp.dot(
-        token_rows,
-        lax.all_gather(flat_weight, "bal", axis=0, tiled=True),
-        preferred_element_type=jnp.float32,
+        token_rows, ring_gather(flat_weight, "bal", 0), preferred_element_type=jnp.float32
     )
     projected = projected.reshape(total_tokens, per_dev_heads, 3, -1)
     query = projected[:, :, 0]

time: 815 us -> 815 us (level)
  waiting for transfers between devices: 554 us -> 433 us
  local copies, waits for them, and re-layouts: 36.1 us -> 119 us
  other arithmetic: 57.9 us -> 76.2 us
  starting transfers between devices: 13.9 us -> 28.6 us
    all_gather x1 -> x0, waiting for transfers between devices: 434 us -> none  [per_device(): lax.all_gather(flat_weight, 'bal', axis=0, tiled=True)]
    ppermute x0 -> x7, waiting for transfers between devices: none -> 378 us  [the longest x4 378 us: ring_gather(): lower.append(lax.ppermute(lower[-1] if lower else x, axis, pairs))]
    all_gather x1, waiting for transfers between devices: 61.3 us -> 0.01 us  [per_device(): whole_tiles = lax.all_gather(compact, 'seq', axis=1, tiled=True)]
    all_to_all x1, waiting for transfers between devices: 58.5 us -> 0.01 us  [per_device(): lax.all_to_all(outbound, 'bal', split_axis=0, concat_axis=0, tiled=True)]
    all_to_all x1, waiting for transfers between devices: 0.01 us -> 54.5 us  [per_device(): lax.all_to_all(filled, 'bal', split_axis=0, concat_axis=0, tiled=True)]
    reshape x0 -> x2, local copies, waits for them, and re-layouts: none -> 33.2 us  [the longest x1 29.6 us: laid_out(): parts.reshape(*shape[:dim], shape[dim] * shape[dim + 1], *shape[dim + 2:])]
    gather x0 -> x3, local copies, waits for them, and re-layouts: none -> 30 us  [ring_gather(): pieces = pieces[(jnp.arange(peers) - shift) % peers]]
    unnamed x1 -> x2, other arithmetic: 0.01 us -> 19.5 us
  transfers between devices with their start and end apart: 4 -> 10, of which waited for: 3 -> 4; matrix products, arithmetic and copies ran while one was open for 4% -> 14% of each run, Pallas kernels for 0% -> 0%
where the time goes in v1:
time: 815 us; the launch traced here: 807 us
  waiting for transfers between devices  433 us (53%)
  local copies, waits for them, and re-layouts  119 us (15%)
  other arithmetic  76.2 us (9%)
  blocking collectives  73.6 us (9%)
  matrix products  62.8 us (8%)
  starting transfers between devices  28.6 us (4%)
  between operations  14.1 us (2%)
    ppermute x4, waiting for transfers between devices, ring_gather(): lower.append(lax.ppermute(lower[-1] if lower else x, axis, pairs))  378 us
    all_to_all x1, waiting for transfers between devices, per_device(): lax.all_to_all(filled, 'bal', split_axis=0, concat_axis=0, tiled=True)  54.5 us
    all_to_all x1, blocking collectives, per_device(): lax.all_to_all(spread_back, 'bal', split_axis=0, concat_axis=0, tiled=True)  45.3 us
    unnamed x51, local copies, waits for them, and re-layouts  36.3 us
    sub x2, other arithmetic, attend(): exp_scores = jnp.exp(scores - largest)  33.9 us
    gather x3, local copies, waits for them, and re-layouts, ring_gather(): pieces = pieces[(jnp.arange(peers) - shift) % peers]  30 us
    dot_general x1, matrix products, per_device(): jnp.dot(token_rows, ring_gather(flat_weight, 'bal', 0), preferred_element...  29.7 us
    reshape x1, local copies, waits for them, and re-layouts, laid_out(): parts.reshape(*shape[:dim], shape[dim] * shape[dim + 1], *shape[dim + 2:])  29.6 us
  transfers between devices with their start and end apart: 10, of which 4 were waited for; matrix products, arithmetic and copies ran while one was open for 14% of the time, Pallas kernels for 0%

profile of v1, /device:TPU:0, one launch (start us, length us, event | category | flops | bytes accessed | tf_op | source)
XLA Modules:
  0.0 806.6 jit_solution(10772905506142008500)
XLA Ops:
  6.5 4.1 copy.87
  18.2 4.9 all-to-all-start
  30.0 54.5 %all-to-all-done = bf16[8,1,2]{2,1,0:T(2,128)(2,1)S(1)} async-done(((bf16[8,1,2]{2,1,0:T(2,128)(2,1)}), bf16[8,1,2]{2,1,0:T(2,128)(2,1)S(1)}, u32[]{:S(2)}, u32[]{:S(2)}) %all-to-all-start) | async-done | bytes 64 | tf_op jit(solution)/shard_map/all_to_all | solution.py:110
  84.5 4.4 all-to-all-start.1
  93.8 149.6 %collective-permute-done.1 = bf16[640,2304]{1,0:T(8,128)(2,1)} collective-permute-done((bf16[640,2304]{1,0:T(8,128)(2,1)}, bf16[640,2304]{1,0:T(8,128)(2,1)}, u32[]{:S(2)}, u32[]{:S(2)}) %collective-permute-start.1) | collective-permute-done | bytes 2949152 | tf_op jit(solution)/shard_map/ppermute | solution.py:25
  256.0 115.6 %collective-permute-done.2 = bf16[640,2304]{1,0:T(8,128)(2,1)} collective-permute-done((bf16[640,2304]{1,0:T(8,128)(2,1)}, bf16[640,2304]{1,0:T(8,128)(2,1)}, u32[]{:S(2)}, u32[]{:S(2)}) %collective-permute-start.2) | collective-permute-done | bytes 2949152 | tf_op jit(solution)/shard_map/ppermute | solution.py:25
  386.1 113.1 %collective-permute-done.3 = bf16[640,2304]{1,0:T(8,128)(2,1)} collective-permute-done((bf16[640,2304]{1,0:T(8,128)(2,1)}, bf16[640,2304]{1,0:T(8,128)(2,1)}, u32[]{:S(2)}, u32[]{:S(2)}) %collective-permute-start.3) | collective-permute-done | bytes 2949152 | tf_op jit(solution)/shard_map/ppermute | solution.py:25
  511.9 8.8 %fusion.52 = (bf16[8,640,1152]{2,1,0:T(8,128)(2,1)}, bf16[8,640,1152]{2,1,0:T(8,128)(2,1)}) fusion(bf16[8,640,2304]{2,1,0:T(8,128)(2,1)S(1)} %bitcast_dynamic-update-slice_fusion), kind=kLoop, calls=%fused_computation.121 | loop fusion | bytes 47185920 | tf_op jit(solution)/shard_map/gather | solution.py:30
  520.8 10.7 %gather_fusion = bf16[8,640,1152]{2,1,0:T(8,128)(2,1)} fusion(bf16[8,640,1152]{2,1,0:T(8,128)(2,1)} %get-tuple-element.15, s32[1024]{0:T(1024)S(1)} %pad_clamp_fusion), kind=kCustom, calls=%fused_computation | custom fusion | bytes 23592992 | tf_op jit(solution)/shard_map/gather | solution.py:30
  531.5 10.5 %gather_fusion.1 = bf16[8,640,1152]{2,1,0:T(8,128)(2,1)} fusion(bf16[8,640,1152]{2,1,0:T(8,128)(2,1)} %get-tuple-element.16, s32[1024]{0:T(1024)S(1)} %pad_clamp_fusion), kind=kCustom, calls=%fused_computation.1 | custom fusion | bytes 23592992 | tf_op jit(solution)/shard_map/gather | solution.py:30
  542.0 19.5 %pad_maximum_fusion = bf16[8,640,2304]{2,1,0:T(8,128)(2,1)} fusion(bf16[8,640,1152]{2,1,0:T(8,128)(2,1)} %gather_fusion.1, bf16[8,640,1152]{2,1,0:T(8,128)(2,1)} %gather_fusion), kind=kLoop, calls=%fused_computation.12 | loop fusion | flops 47185920 | bytes 47185920
  561.4 29.6 %copy.92 = bf16[5120,2304]{0,1:T(8,128)(2,1)} copy(bf16[5120,2304]{1,0:T(8,128)(2,1)} %bitcast.85) | data formatting | bytes 47185920 | tf_op jit(solution)/shard_map/reshape | solution.py:15
  591.1 5.6 convert_reduce_fusion
  600.9 8.2 %fusion.7 = bf16[16,64,5120]{2,1,0:T(8,128)(2,1)} fusion(bf16[16,64,5120]{2,1,0:T(8,128)(2,1)S(1)} %copy-done, f32[16,5120]{1,0:T(8,128)S(1)} %get-tuple-element.18, f32[16,5120]{1,0:T(8,128)S(1)} %get-tuple-element.17, f32[16,64]{1,0:T(8,128)S(1)} %add_rsqrt_fusion, f32[16,64]{1,0:T(8,128)S(1)} %broadcast_multiply_fusion), kind=kLoop, calls=%fused_computation.16 | loop fusion | flops 31457280 | bytes 21635072 | tf_op jit(solution)/shard_map/convert_element_type | solution.py:77
  609.1 29.7 %fusion.56 = f32[1024,6,3,128]{0,3,2,1:T(8,128)S(1)} fusion(bf16[1024,5120,1,1]{1,0,3,2:T(8,128)(2,1)} %bitcast.91, bf16[6,3,128,5120]{3,2,1,0:T(8,128)(2,1)} %bitcast.90), kind=kOutput, calls=%fused_computation.125 | convolution fusion | flops 24159191040 | bytes 43515904 | tf_op jit(solution)/shard_map/dot_general | solution.py:129
  643.1 5.8 all-reduce
  651.3 8.4 %fusion.25 = f32[6,512,1024]{2,1,0:T(8,128)} fusion(bf16[1024,6,128]{0,2,1:T(8,128)(2,1)S(1)} %multiply_convert_fusion.1, f32[1024,6,3,128]{0,3,2,1:T(8,128)} %copy-done.1, f32[6,128]{1,0:T(8,128)S(1)} %copy-done.5, f32[1024]{0:T(1024)S(1)} %get-tuple-element.29), kind=kOutput, calls=%fused_computation.56 | convolution fusion | flops 807665664 | bytes 16523264 | tf_op jit(solution)/shard_map/qhd,khd->hqk/dot_general | solution.py:81
  659.8 6.5 fusion.23
  666.2 17.4 %fusion.55 = (f32[6,512]{1,0:T(8,128)S(1)}, f32[6,512,1024]{2,1,0:T(8,128)}) fusion(f32[6,512,1024]{2,1,0:T(8,128)} %fusion.25, pred[512,1024]{1,0:T(8,128)(4,1)S(1)} %copy.93), kind=kOutput, calls=%fused_computation.124 | output fusion | flops 18875392 | bytes 25702400 | tf_op jit(solution)/shard_map/sub | solution.py:86
  683.6 7.0 fusion.21
  690.6 16.5 %fusion.54 = (f32[6,512]{1,0:T(8,128)S(1)}, f32[6,512,1024]{2,1,0:T(8,128)}) fusion(f32[6,512,1024]{2,1,0:T(8,128)} %fusion.23, pred[512,1024]{1,0:T(8,128)(4,1)S(1)} %copy-done.3), kind=kOutput, calls=%fused_computation.123 | output fusion | flops 18875392 | bytes 25702400 | tf_op jit(solution)/shard_map/sub | solution.py:86
  707.1 6.9 fusion.22
  725.5 45.3 %all_to_all.35 = bf16[8,2,64,768]{3,1,2,0:T(2,128)(2,1)S(1)} all-to-all(bf16[8,2,64,768]{3,1,2,0:T(2,128)(2,1)S(1)} %copy.100), channel_id=1, replica_groups=mesh['bal'=8,'seq'=4] {'bal'}, dimensions={0} | all-to-all | bytes 3145728 | tf_op jit(solution)/shard_map/all_to_all | solution.py:165
  771.9 22.5 %all_to_all.36 = bf16[8,2,64,768]{3,1,0,2:T(2,128)(2,1)S(1)} all-to-all(bf16[8,2,64,768]{3,1,0,2:T(2,128)(2,1)S(1)} %copy.101), channel_id=1, replica_groups=mesh['bal'=8,'seq'=4] {'seq'}, dimensions={2} | all-to-all | bytes 3145728 | tf_op jit(solution)/shard_map/all_to_all | solution.py:164
  (119 shorter events, 87.3 us)
Async XLA Ops:
  6.5 10.7 %copy-start.14 = (s32[16]{0:T(128)S(1)}, s32[16]{0:T(128)}, u32[]{:S(2)}) copy-start(s32[16]{0:T(128)} %param.12) | copy-start | bytes 196
  14.3 74.8 %collective-permute-start = (bf16[640,2304]{1,0:T(8,128)(2,1)}, bf16[640,2304]{1,0:T(8,128)(2,1)}, u32[]{:S(2)}, u32[]{:S(2)}) collective-permute-start(bf16[640,2304]{1,0:T(8,128)(2,1)} %copy.88), channel_id=1, source_target_pairs={{0,4},{4,8},{8,12},{12,16},{16,20},{20,24},{24,28},{28,0},{1,5},{5... | collective-permute-start | bytes 8847368 | tf_op jit(solution)/shard_map/ppermute | solution.py:25
  17.4 67.1 %copy-start.11 = (s32[16]{0:T(128)}, s32[16]{0:T(128)S(1)}, u32[]{:S(2)}) copy-start(s32[16]{0:T(128)S(1)} %multiply_add_fusion) | copy-start | bytes 196
  18.2 66.3 %all-to-all-start = ((bf16[8,1,2]{2,1,0:T(2,128)(2,1)}), bf16[8,1,2]{2,1,0:T(2,128)(2,1)S(1)}, u32[]{:S(2)}, u32[]{:S(2)}) async-start(bf16[8,1,2]{2,1,0:T(2,128)(2,1)} %all_to_all.30), calls=%async_computation | async-start | bytes 8192 | tf_op jit(solution)/shard_map/all_to_all | solution.py:110
  84.5 161.7 %all-to-all-start.1 = ((bf16[8,2,16,5120]{3,2,1,0:T(8,128)(2,1)}), bf16[8,2,16,5120]{3,2,1,0:T(8,128)(2,1)}, u32[]{:S(2)}, u32[]{:S(2)}) async-start(bf16[8,2,16,5120]{3,2,1,0:T(8,128)(2,1)} %bitcast.93), calls=%async_computation.1 | async-start | bytes 5242880 | tf_op jit(solution)/shard_map/all_to_all | solution.py:109
  89.0 164.3 %copy-start.13 = (s32[1,4,3]{1,0,2:T(1,128)S(1)}, s32[1,4,3]{1,0,2:T(1,128)}, u32[]{:S(2)}) copy-start(s32[1,4,3]{1,0,2:T(1,128)} %param.13) | copy-start | bytes 148
  89.0 502.1 %all-gather.2.cloned.1.call-start = ((), (), s32[]{:S(2)}) async-start(), calls=%async_computation.4 | async-start | bytes 13107200 | tf_op jit(solution)/shard_map/all_gather | solution.py:123
  89.0 154.4 %collective-permute-start.1 = (bf16[640,2304]{1,0:T(8,128)(2,1)}, bf16[640,2304]{1,0:T(8,128)(2,1)}, u32[]{:S(2)}, u32[]{:S(2)}) collective-permute-start(bf16[640,2304]{1,0:T(8,128)(2,1)} %collective-permute-done), channel_id=1, source_target_pairs={{0,4},{4,8},{8,12},{12,16},{16,20},{20,24},{24,28},{28,0},{1,5},{5... | collective-permute-start | bytes 8847368 | tf_op jit(solution)/shard_map/ppermute | solution.py:25
  90.9 162.5 %collective-permute-start.4 = (bf16[640,2304]{1,0:T(8,128)(2,1)}, bf16[640,2304]{1,0:T(8,128)(2,1)}, u32[]{:S(2)}, u32[]{:S(2)}) collective-permute-start(bf16[640,2304]{1,0:T(8,128)(2,1)} %copy.88), channel_id=1, source_target_pairs={{4,0},{8,4},{12,8},{16,12},{20,16},{24,20},{28,24},{0,28},{5,1},{9... | collective-permute-start | bytes 8847368 | tf_op jit(solution)/shard_map/ppermute | solution.py:27
  243.4 128.2 %collective-permute-start.2 = (bf16[640,2304]{1,0:T(8,128)(2,1)}, bf16[640,2304]{1,0:T(8,128)(2,1)}, u32[]{:S(2)}, u32[]{:S(2)}) collective-permute-start(bf16[640,2304]{1,0:T(8,128)(2,1)} %collective-permute-done.1), channel_id=1, source_target_pairs={{0,4},{4,8},{8,12},{12,16},{16,20},{20,24},{24,28},{28,0},{1,5},{5... | collective-permute-start | bytes 8847368 | tf_op jit(solution)/shard_map/ppermute | solution.py:25
  250.3 131.7 %copy-start.4 = (f32[1,4,2,5120]{3,2,1,0:T(2,128)S(1)}, f32[1,4,2,5120]{3,2,1,0:T(2,128)}, u32[]{:S(2)}) copy-start(f32[1,4,2,5120]{3,2,1,0:T(2,128)} %param.11) | copy-start | bytes 491524
  253.4 128.9 %collective-permute-start.5 = (bf16[640,2304]{1,0:T(8,128)(2,1)}, bf16[640,2304]{1,0:T(8,128)(2,1)}, u32[]{:S(2)}, u32[]{:S(2)}) collective-permute-start(bf16[640,2304]{1,0:T(8,128)(2,1)} %collective-permute-done.4), channel_id=1, source_target_pairs={{4,0},{8,4},{12,8},{16,12},{20,16},{24,20},{28,24},{0,28},{5,1},{9... | collective-permute-start | bytes 8847368 | tf_op jit(solution)/shard_map/ppermute | solution.py:27
  371.6 127.5 %collective-permute-start.3 = (bf16[640,2304]{1,0:T(8,128)(2,1)}, bf16[640,2304]{1,0:T(8,128)(2,1)}, u32[]{:S(2)}, u32[]{:S(2)}) collective-permute-start(bf16[640,2304]{1,0:T(8,128)(2,1)} %collective-permute-done.2), channel_id=1, source_target_pairs={{0,4},{4,8},{8,12},{12,16},{16,20},{20,24},{24,28},{28,0},{1,5},{5... | collective-permute-start | bytes 8847368 | tf_op jit(solution)/shard_map/ppermute | solution.py:25
  382.3 129.4 %collective-permute-start.6 = (bf16[640,2304]{1,0:T(8,128)(2,1)}, bf16[640,2304]{1,0:T(8,128)(2,1)S(1)}, u32[]{:S(2)}, u32[]{:S(2)}) collective-permute-start(bf16[640,2304]{1,0:T(8,128)(2,1)} %collective-permute-done.5), channel_id=1, source_target_pairs={{4,0},{8,4},{12,8},{16,12},{20,16},{24,20},{28,24},{0,28},{5,1},{9... | collective-permute-start | bytes 8847368 | tf_op jit(solution)/shard_map/ppermute | solution.py:27
  591.1 7.0 copy-start
  609.1 39.8 %copy-start.8 = (f32[6,128]{1,0:T(8,128)S(1)}, f32[6,128]{1,0:T(8,128)}, u32[]{:S(2)}) copy-start(f32[6,128]{1,0:T(8,128)} %param.9) | copy-start | bytes 9220
  642.5 8.8 %copy-start.5 = (f32[6,128]{1,0:T(8,128)S(1)}, f32[6,128]{1,0:T(8,128)}, u32[]{:S(2)}) copy-start(f32[6,128]{1,0:T(8,128)} %param.10) | copy-start | bytes 9220
  648.9 10.8 %slice-start = ((s8[9437184]{0:T(1024)(128)(4,1)}), s8[4194304]{0:T(1024)(128)(4,1)S(1)}, s32[]{:S(2)}) async-start(s8[9437184]{0:T(1024)(128)(4,1)} %bitcast.88), calls=%async_computation.5 | async-start | bytes 8388608
  651.3 8.4 %slice-start.1 = ((s8[9437184]{0:T(1024)(128)(4,1)}), s8[4194304]{0:T(1024)(128)(4,1)S(1)}, s32[]{:S(2)}) async-start(s8[9437184]{0:T(1024)(128)(4,1)} %bitcast.88), calls=%async_computation.6 | async-start | bytes 8388608
  651.3 8.4 %slice-start.2 = ((s8[9437184]{0:T(1024)(128)(4,1)}), s8[1048576]{0:T(1024)(128)(4,1)S(1)}, s32[]{:S(2)}) async-start(s8[9437184]{0:T(1024)(128)(4,1)} %bitcast.88), calls=%async_computation.7 | async-start | bytes 2097152
  683.6 7.0 copy-start.3
  714.0 7.5 copy-start.7
  714.1 7.5 copy-start.10
  725.5 71.4 %copy-start.12 = (s32[16]{0:T(128)S(1)}, s32[16]{0:T(128)}, u32[]{:S(2)}) copy-start(s32[16]{0:T(128)} %copy-done.11) | copy-start | bytes 196
  (4 other events, 16.4 us)
Sparse Core Ops, SparseCore 0:
  253.4 69.8 all-gather.1
